TPU v7x, 32 devices: a whole 2x2x4 slice. The times are simulated.
32 devices in a mesh: shot: 4 (over z), gx: 4 (over x, core), gy: 2 (over y).
Axes of the slice: x: 2, y: 2, z: 4, core: 2. Of those that a mesh axis runs over, the one named last changes fastest.
Arguments:
- partials: float32 [4, 9, 4, 32, 256], P('shot', None, None, 'gx', 'gy'), may hold values from -16 to 16, as said below
- hist_s: float32 [5, 3, 4, 32, 256], P(None, None, 'shot', 'gx', 'gy'), may hold values from -30 to 30
- hist_y: float32 [5, 3, 4, 32, 256], P(None, None, 'shot', 'gx', 'gy'), may hold values from -70 to 70, as said below
Outputs:
- direction: float32 [3, 4, 32, 256], P(None, 'shot', 'gx', 'gy')
Inputs may be any that keep to these rules, and one draw needn't show every extreme that they name: `partials`: for every shot group and cell, entries 3, 4, 5 are positive and each exceeds the sum of the magnitudes of the two off-diagonal entries of its row of the 3x3 matrix [[e3, e6, e7], [e6, e4, e8], [e7, e8, e5]]. Each entry of hist_y times the matching entry of hist_s is at least 0.2 times the square of that hist_s entry.
All inputs are finite; a program needn't handle non-finite values.
Results may differ from a plain program's by a relative error of at most 0.00013.
Values sent between devices are 32-bit elements; how exact they have to be, the bound alone decides.
No kernel may reach another device: no remote copies, remote signals or barrier semaphores. Data moves between devices by JAX's collectives and lax.ppermute only.
A program may use at most 64 MiB of HBM per device.

v0:
```python
import jax
import jax.numpy as jnp
from jax import lax
from jax.sharding import PartitionSpec as P

PAIRS = 5


def extended_2(cells, sides, width):
    for axis, dim in sides:
        count = lax.axis_size(axis)
        ends = count - 1
        head = lax.slice_in_dim(cells, 0, width, axis=dim)
        tail = lax.slice_in_dim(cells, cells.shape[dim] - width, cells.shape[dim], axis=dim)
        cells = jnp.concatenate(
            [
                lax.ppermute(tail, axis, [(i, (i + 1) % count) for i in range(ends)]),
                cells,
                lax.ppermute(head, axis, [((i + 1) % count, i) for i in range(ends)]),
            ],
            axis=dim,
        )
    return cells


def smooth_block(padded):
    along_x = 0.25 * (padded[:, :, :-2] + 2.0 * padded[:, :, 1:-1] + padded[:, :, 2:])
    return 0.25 * (along_x[..., :-2] + 2.0 * along_x[..., 1:-1] + along_x[..., 2:])


def apply_inverse(hessian, vectors):
    diag_p = hessian[0]
    diag_s = hessian[1]
    diag_r = hessian[2]
    cross_ps = hessian[3]
    cross_pr = hessian[4]
    cross_sr = hessian[5]
    cof_pp = diag_s * diag_r - cross_sr * cross_sr
    cof_ps = cross_pr * cross_sr - cross_ps * diag_r
    cof_pr = cross_ps * cross_sr - diag_s * cross_pr
    cof_ss = diag_p * diag_r - cross_pr * cross_pr
    cof_sr = cross_ps * cross_pr - diag_p * cross_sr
    cof_rr = diag_p * diag_s - cross_ps * cross_ps
    determinant = diag_p * cof_pp + cross_ps * cof_ps + cross_pr * cof_pr
    inverse_det = 1.0 / determinant
    comp_one = vectors[:, 0]
    comp_two = vectors[:, 1]
    comp_three = vectors[:, 2]
    return jnp.stack(
        [
            (cof_pp * comp_one + cof_ps * comp_two + cof_pr * comp_three) * inverse_det,
            (cof_ps * comp_one + cof_ss * comp_two + cof_sr * comp_three) * inverse_det,
            (cof_pr * comp_one + cof_sr * comp_two + cof_rr * comp_three) * inverse_det,
        ],
        axis=1,
    )


def pair_dots(left_flat, right_flat):
    return lax.dot_general(
        left_flat,
        right_flat,
        (((1,), (1,)), ((), ())),
        precision=lax.Precision.HIGHEST,
        preferred_element_type=jnp.float32,
    )


def upper_solve(matrix, values):
    count = matrix.shape[0]
    found = [None] * count
    for row in range(count - 1, -1, -1):
        total = values[row]
        for col in range(row + 1, count):
            total = total - matrix[row, col] * found[col]
        found[row] = total / matrix[row, row]
    return jnp.stack(found)


def upper_transpose_solve(matrix, values):
    count = matrix.shape[0]
    found = [None] * count
    for row in range(count):
        total = values[row]
        for col in range(row):
            total = total - matrix[col, row] * found[col]
        found[row] = total / matrix[row, row]
    return jnp.stack(found)


def combine_terms(cross_gram, curv_gram, hist_dot, pre_dot, solved, hist_s):
    middle_part = jnp.diag(jnp.diag(cross_gram)) + curv_gram
    coef_p = upper_solve(cross_gram, hist_dot)
    right_hand = jnp.dot(middle_part, coef_p, precision=lax.Precision.HIGHEST) - pre_dot
    coef_q = upper_transpose_solve(cross_gram, right_hand)
    update_s = jnp.tensordot(coef_q, hist_s, axes=1, precision=lax.Precision.HIGHEST)
    update_z = jnp.tensordot(coef_p, solved[1:], axes=1, precision=lax.Precision.HIGHEST)
    return -(solved[0] + update_s - update_z)


def per_device(partials, hist_s, hist_y):
    s_flat = hist_s.reshape(PAIRS, -1)
    y_flat = hist_y.reshape(PAIRS, -1)
    inverse_count = 1.0 / lax.axis_size("shot")
    level_sums = lax.psum_scatter(partials[0], "shot", scatter_dimension=1, tiled=True)
    fields = level_sums * inverse_count
    extended = extended_2(fields, (("gx", 2), ("gy", 3)), 1)
    smoothed = smooth_block(extended)
    gradient = smoothed[0:3]
    solved = apply_inverse(smoothed[3:9], jnp.concatenate([gradient[None], hist_y], axis=0))
    z_flat = solved[1:].reshape(PAIRS, -1)
    curv_part = pair_dots(y_flat, z_flat)
    hist_part = pair_dots(s_flat, gradient.reshape(1, -1))[:, 0]
    pre_part = pair_dots(y_flat, solved[0].reshape(1, -1))[:, 0]
    cross_gram, curv_gram, hist_dot, pre_dot = lax.psum(
        (pair_dots(s_flat, y_flat), curv_part, hist_part, pre_part), ("shot", "gx", "gy")
    )
    return combine_terms(cross_gram, curv_gram, hist_dot, pre_dot, solved, hist_s)


def solution(mesh):
    return jax.shard_map(
        per_device,
        mesh=mesh,
        in_specs=(
            P("shot", None, None, "gx", "gy"),
            P(None, None, "shot", "gx", "gy"),
            P(None, None, "shot", "gx", "gy"),
        ),
        out_specs=P(None, "shot", "gx", "gy"),
        check_vma=False,
    )
```

profile of v0, /device:TPU:14, one launch (start us, length us, event | category | flops | bytes accessed | tf_op | source)
XLA Modules:
  0.0 124.9 jit_solution(4067416101223130220)
XLA Ops:
  6.5 0.0 reduce-scatter.4.cloned.1.call-start
  6.5 1.6 %copy.40 = f32[1,9,4,8,128]{4,3,1,2,0:T(8,128)} copy(f32[1,9,4,8,128]{4,3,2,1,0:T(8,128)} %param.3) | data formatting | bytes 294912 | tf_op args[0]
  8.1 0.0 reduce-scatter.4.cloned.1.call-update
  8.1 19.2 %reduce-scatter.4.cloned.1.call-done = f32[9,1,8,128]{3,2,0,1:T(8,128)} async-done(((f32[9,4,8,128]{3,2,0,1:T(8,128)}), f32[9,1,8,128]{3,2,0,1:T(8,128)}) %reduce-scatter.4.cloned.1.call-update) | async-done | bytes 36880
  27.4 0.8 broadcast_multiply_fusion
  28.2 1.9 %collective-permute-start = (f32[9,1,1,128]{3,2,0,1:T(1,128)S(1)}, f32[9,1,1,128]{3,2,0,1:T(1,128)S(1)}, u32[]{:S(2)}, u32[]{:S(2)}) collective-permute-start(f32[9,1,1,128]{3,2,0,1:T(1,128)S(1)} %get-tuple-element.25), channel_id=1, source_target_pairs={{0,2},{2,4},{4,6},{1,3},{3,5},{5,7},{8,10},{10,12},{12,14},{9,11},... | collective-permute-start | bytes 13832 | tf_op jit(solution)/shard_map/ppermute | solution.py:17
  30.1 3.6 %collective-permute-start.1 = (f32[9,1,1,128]{3,2,0,1:T(1,128)S(1)}, f32[9,1,1,128]{3,2,0,1:T(1,128)S(1)}, u32[]{:S(2)}, u32[]{:S(2)}) collective-permute-start(f32[9,1,1,128]{3,2,0,1:T(1,128)S(1)} %get-tuple-element.26), channel_id=1, source_target_pairs={{2,0},{4,2},{6,4},{3,1},{5,3},{7,5},{10,8},{12,10},{14,12},{11,9},... | collective-permute-start | bytes 13832 | tf_op jit(solution)/shard_map/ppermute | solution.py:19
  33.7 0.0 collective-permute-done
  33.8 1.3 %collective-permute-done.1 = f32[9,1,1,128]{3,2,0,1:T(1,128)S(1)} collective-permute-done((f32[9,1,1,128]{3,2,0,1:T(1,128)S(1)}, f32[9,1,1,128]{3,2,0,1:T(1,128)S(1)}, u32[]{:S(2)}, u32[]{:S(2)}) %collective-permute-start.1) | collective-permute-done | bytes 4640 | tf_op jit(solution)/shard_map/ppermute | solution.py:19
  35.1 0.0 copy-start
  35.1 0.0 copy-start.1
  35.1 0.1 fusion.26
  35.2 1.3 %collective-permute-start.2 = (f32[9,1,10,1]{3,2,0,1:T(8,128)S(1)}, f32[9,1,10,1]{3,2,0,1:T(8,128)S(1)}, u32[]{:S(2)}, u32[]{:S(2)}) collective-permute-start(f32[9,1,10,1]{3,2,0,1:T(8,128)S(1)} %get-tuple-element.16), channel_id=1, source_target_pairs={{0,1},{2,3},{4,5},{6,7},{8,9},{10,11},{12,13},{14,15},{16,17},{18,... | collective-permute-start | bytes 1088 | tf_op jit(solution)/shard_map/ppermute | solution.py:17
  36.5 4.5 %collective-permute-start.3 = (f32[9,1,10,1]{3,2,0,1:T(8,128)S(1)}, f32[9,1,10,1]{3,2,0,1:T(8,128)S(1)}, u32[]{:S(2)}, u32[]{:S(2)}) collective-permute-start(f32[9,1,10,1]{3,2,0,1:T(8,128)S(1)} %get-tuple-element.17), channel_id=1, source_target_pairs={{1,0},{3,2},{5,4},{7,6},{9,8},{11,10},{13,12},{15,14},{17,16},{19,... | collective-permute-start | bytes 1088 | tf_op jit(solution)/shard_map/ppermute | solution.py:19
  41.0 0.0 copy-done
  41.0 0.0 copy-done.1
  41.1 0.3 convolution_bitcast_fusion.1
  41.3 0.1 copy.13
  41.4 0.0 collective-permute-done.2
  41.4 1.6 %collective-permute-done.3 = f32[9,1,10,1]{3,2,0,1:T(8,128)S(1)} collective-permute-done((f32[9,1,10,1]{3,2,0,1:T(8,128)S(1)}, f32[9,1,10,1]{3,2,0,1:T(8,128)S(1)}, u32[]{:S(2)}, u32[]{:S(2)}) %collective-permute-start.3) | collective-permute-done | bytes 392 | tf_op jit(solution)/shard_map/ppermute | solution.py:19
  43.0 0.2 pad_maximum_fusion
  43.2 0.1 fusion.12
  43.4 0.3 convolution_bitcast_fusion
  43.7 0.1 pad_maximum_fusion.5
  43.8 0.3 convolution_bitcast_fusion.4
  44.0 0.3 convolution_bitcast_fusion.3
  44.4 0.1 or_bitcast_fusion
  44.4 43.8 %all-reduce.1 = (f32[5]{0:T(128)S(1)}, f32[5,5]{1,0:T(8,128)S(1)}, f32[5]{0:T(128)S(1)}, f32[5,5]{0,1:T(8,128)S(1)}) all-reduce(f32[5]{0:T(128)S(1)} %convolution_bitcast_fusion.4, f32[5,5]{1,0:T(8,128)S(1)} %convolution_bitcast_fusion.1, ...), channel_id=1, replica_groups=mesh['shot'=4,'gx'=4,'gy'=2] {'shot','gx','gy'}, use_global_device_ids=true, to_apply=%region_3.0 | all-reduce | flops 60 | bytes 480 | tf_op jit(solution)/shard_map/psum | solution.py:115
  88.3 0.7 fusion.28
  89.0 0.7 fusion.30
  99.2 0.6 gather_fusion
  103.1 0.1 stack.48
  103.2 0.1 fusion
  103.3 0.7 fusion.29
  116.9 0.1 stack.54
  116.9 0.2 fusion.1
  117.2 0.2 fusion.21
  117.4 0.6 negate_bitcast_fusion
  (8 shorter events, 0.2 us)
Async XLA Ops:
  6.5 20.8 %reduce-scatter.4.cloned.1.call-start = ((), (), s32[]{:S(2)}) async-start(), calls=%async_computation.1 | async-start | bytes 184320
  28.2 5.6 %collective-permute-start = (f32[9,1,1,128]{3,2,0,1:T(1,128)S(1)}, f32[9,1,1,128]{3,2,0,1:T(1,128)S(1)}, u32[]{:S(2)}, u32[]{:S(2)}) collective-permute-start(f32[9,1,1,128]{3,2,0,1:T(1,128)S(1)} %get-tuple-element.25), channel_id=1, source_target_pairs={{0,2},{2,4},{4,6},{1,3},{3,5},{5,7},{8,10},{10,12},{12,14},{9,11},... | collective-permute-start | bytes 13832 | tf_op jit(solution)/shard_map/ppermute | solution.py:17
  30.1 5.0 %collective-permute-start.1 = (f32[9,1,1,128]{3,2,0,1:T(1,128)S(1)}, f32[9,1,1,128]{3,2,0,1:T(1,128)S(1)}, u32[]{:S(2)}, u32[]{:S(2)}) collective-permute-start(f32[9,1,1,128]{3,2,0,1:T(1,128)S(1)} %get-tuple-element.26), channel_id=1, source_target_pairs={{2,0},{4,2},{6,4},{3,1},{5,3},{7,5},{10,8},{12,10},{14,12},{11,9},... | collective-permute-start | bytes 13832 | tf_op jit(solution)/shard_map/ppermute | solution.py:19
  35.1 6.0 %copy-start = (f32[5,3,1,8,128]{4,3,2,1,0:T(8,128)S(1)}, f32[5,3,1,8,128]{4,3,2,1,0:T(8,128)}, u32[]{:S(2)}) copy-start(f32[5,3,1,8,128]{4,3,2,1,0:T(8,128)} %param.5) | copy-start | bytes 184324
  35.1 6.0 %copy-start.1 = (f32[5,3,1,8,128]{4,3,2,1,0:T(8,128)S(1)}, f32[5,3,1,8,128]{4,3,2,1,0:T(8,128)}, u32[]{:S(2)}) copy-start(f32[5,3,1,8,128]{4,3,2,1,0:T(8,128)} %param.4) | copy-start | bytes 184324
  35.2 6.2 %collective-permute-start.2 = (f32[9,1,10,1]{3,2,0,1:T(8,128)S(1)}, f32[9,1,10,1]{3,2,0,1:T(8,128)S(1)}, u32[]{:S(2)}, u32[]{:S(2)}) collective-permute-start(f32[9,1,10,1]{3,2,0,1:T(8,128)S(1)} %get-tuple-element.16), channel_id=1, source_target_pairs={{0,1},{2,3},{4,5},{6,7},{8,9},{10,11},{12,13},{14,15},{16,17},{18,... | collective-permute-start | bytes 1088 | tf_op jit(solution)/shard_map/ppermute | solution.py:17
  36.5 6.5 %collective-permute-start.3 = (f32[9,1,10,1]{3,2,0,1:T(8,128)S(1)}, f32[9,1,10,1]{3,2,0,1:T(8,128)S(1)}, u32[]{:S(2)}, u32[]{:S(2)}) collective-permute-start(f32[9,1,10,1]{3,2,0,1:T(8,128)S(1)} %get-tuple-element.17), channel_id=1, source_target_pairs={{1,0},{3,2},{5,4},{7,6},{9,8},{11,10},{13,12},{15,14},{17,16},{19,... | collective-permute-start | bytes 1088 | tf_op jit(solution)/shard_map/ppermute | solution.py:19
Sparse Core Ops, SparseCore 0:
  9.6 17.7 reduce-scatter.3
where the time goes:
time: 126 us; the launch traced here: 125 us
  blocking collectives  43.8 us (35%)
  between operations  39.2 us (31%)
  waiting for transfers between devices  22.1 us (18%)
  starting transfers between devices  11.4 us (9%)
  local copies, waits for them, and re-layouts  4.65 us (4%)
  other arithmetic  1.9 us (2%)
  matrix products  1.73 us (1%)
    psum x1, blocking collectives, per_device(): lax.psum((pair_dots(s_flat, y_flat), curv_part, hist_part, pre_part), ('s...  43.8 us
    unnamed x2, waiting for transfers between devices  19.3 us
    ppermute x2, starting transfers between devices, extended_2(): lax.ppermute(head, axis, [((i + 1) % count, i) for i in range(ends)])  8.19 us
    ppermute x2, starting transfers between devices, extended_2(): lax.ppermute(tail, axis, [(i, (i + 1) % count) for i in range(ends)])  3.21 us
    ppermute x2, waiting for transfers between devices, extended_2(): lax.ppermute(head, axis, [((i + 1) % count, i) for i in range(ends)])  2.87 us
  transfers between devices with their start and end apart: 5, of which 3 were waited for; matrix products, arithmetic and copies ran while one was open for 0% of the time, Pallas kernels for 0%

commit v1 on v0

--- a/solution.py
+++ b/solution.py
@@ -2,6 +2,7 @@
 import jax.numpy as jnp
 from jax import lax
 from jax.sharding import PartitionSpec as P
+from jax.lax import psum
 
 PAIRS = 5
 
@@ -99,6 +100,10 @@
 
 
 def per_device(partials, hist_s, hist_y):
+
+    def threads_convert(vec, peer_axis, axis_name):
+        return psum(psum(vec, peer_axis), axis_name)
+
     s_flat = hist_s.reshape(PAIRS, -1)
     y_flat = hist_y.reshape(PAIRS, -1)
     inverse_count = 1.0 / lax.axis_size("shot")
@@ -112,8 +117,8 @@
     curv_part = pair_dots(y_flat, z_flat)
     hist_part = pair_dots(s_flat, gradient.reshape(1, -1))[:, 0]
     pre_part = pair_dots(y_flat, solved[0].reshape(1, -1))[:, 0]
-    cross_gram, curv_gram, hist_dot, pre_dot = lax.psum(
-        (pair_dots(s_flat, y_flat), curv_part, hist_part, pre_part), ("shot", "gx", "gy")
+    cross_gram, curv_gram, hist_dot, pre_dot = threads_convert(
+        (pair_dots(s_flat, y_flat), curv_part, hist_part, pre_part), ("gx", "gy"), "shot"
     )
     return combine_terms(cross_gram, curv_gram, hist_dot, pre_dot, solved, hist_s)
 

time: 126 us -> 109 us (0.87)
  blocking collectives: 43.8 us -> 27.2 us
    psum x1 -> x2, blocking collectives: 43.8 us -> 27.2 us  [threads_convert(): return psum(psum(vec, peer_axis), axis_name)]
where the time goes in v1:
time: 109 us; the launch traced here: 108 us
  between operations  39.1 us (36%)
  blocking collectives  27.2 us (25%)
  waiting for transfers between devices  22.2 us (20%)
  starting transfers between devices  11.4 us (10%)
  local copies, waits for them, and re-layouts  4.64 us (4%)
  other arithmetic  1.9 us (2%)
  matrix products  1.72 us (2%)
    psum x2, blocking collectives, threads_convert(): return psum(psum(vec, peer_axis), axis_name)  27.2 us
    unnamed x2, waiting for transfers between devices  19.3 us
    ppermute x2, starting transfers between devices, extended_2(): lax.ppermute(head, axis, [((i + 1) % count, i) for i in range(ends)])  8.19 us
    ppermute x2, starting transfers between devices, extended_2(): lax.ppermute(tail, axis, [(i, (i + 1) % count) for i in range(ends)])  3.21 us
    ppermute x2, waiting for transfers between devices, extended_2(): lax.ppermute(head, axis, [((i + 1) % count, i) for i in range(ends)])  2.87 us
  transfers between devices with their start and end apart: 5, of which 3 were waited for; matrix products, arithmetic and copies ran while one was open for 0% of the time, Pallas kernels for 0%

profile of v1, /device:TPU:14, one launch (start us, length us, event | category | flops | bytes accessed | tf_op | source)
XLA Modules:
  0.0 108.1 jit_solution(15997432623930500243)
XLA Ops:
  6.5 0.0 reduce-scatter.4.cloned.1.call-start
  6.5 1.6 %copy.40 = f32[1,9,4,8,128]{4,3,1,2,0:T(8,128)} copy(f32[1,9,4,8,128]{4,3,2,1,0:T(8,128)} %param.3) | data formatting | bytes 294912 | tf_op args[0]
  8.1 0.0 reduce-scatter.4.cloned.1.call-update
  8.1 19.2 %reduce-scatter.4.cloned.1.call-done = f32[9,1,8,128]{3,2,0,1:T(8,128)} async-done(((f32[9,4,8,128]{3,2,0,1:T(8,128)}), f32[9,1,8,128]{3,2,0,1:T(8,128)}) %reduce-scatter.4.cloned.1.call-update) | async-done | bytes 36880
  27.4 0.8 broadcast_multiply_fusion
  28.2 1.9 %collective-permute-start = (f32[9,1,1,128]{3,2,0,1:T(1,128)S(1)}, f32[9,1,1,128]{3,2,0,1:T(1,128)S(1)}, u32[]{:S(2)}, u32[]{:S(2)}) collective-permute-start(f32[9,1,1,128]{3,2,0,1:T(1,128)S(1)} %get-tuple-element.29), channel_id=1, source_target_pairs={{0,2},{2,4},{4,6},{1,3},{3,5},{5,7},{8,10},{10,12},{12,14},{9,11},... | collective-permute-start | bytes 13832 | tf_op jit(solution)/shard_map/ppermute | solution.py:18
  30.1 3.6 %collective-permute-start.1 = (f32[9,1,1,128]{3,2,0,1:T(1,128)S(1)}, f32[9,1,1,128]{3,2,0,1:T(1,128)S(1)}, u32[]{:S(2)}, u32[]{:S(2)}) collective-permute-start(f32[9,1,1,128]{3,2,0,1:T(1,128)S(1)} %get-tuple-element.30), channel_id=1, source_target_pairs={{2,0},{4,2},{6,4},{3,1},{5,3},{7,5},{10,8},{12,10},{14,12},{11,9},... | collective-permute-start | bytes 13832 | tf_op jit(solution)/shard_map/ppermute | solution.py:20
  33.7 0.0 collective-permute-done
  33.8 1.3 %collective-permute-done.1 = f32[9,1,1,128]{3,2,0,1:T(1,128)S(1)} collective-permute-done((f32[9,1,1,128]{3,2,0,1:T(1,128)S(1)}, f32[9,1,1,128]{3,2,0,1:T(1,128)S(1)}, u32[]{:S(2)}, u32[]{:S(2)}) %collective-permute-start.1) | collective-permute-done | bytes 4640 | tf_op jit(solution)/shard_map/ppermute | solution.py:20
  35.1 0.0 copy-start
  35.1 0.0 copy-start.1
  35.1 0.1 fusion.26
  35.2 1.3 %collective-permute-start.2 = (f32[9,1,10,1]{3,2,0,1:T(8,128)S(1)}, f32[9,1,10,1]{3,2,0,1:T(8,128)S(1)}, u32[]{:S(2)}, u32[]{:S(2)}) collective-permute-start(f32[9,1,10,1]{3,2,0,1:T(8,128)S(1)} %get-tuple-element.20), channel_id=1, source_target_pairs={{0,1},{2,3},{4,5},{6,7},{8,9},{10,11},{12,13},{14,15},{16,17},{18,... | collective-permute-start | bytes 1088 | tf_op jit(solution)/shard_map/ppermute | solution.py:18
  36.5 4.5 %collective-permute-start.3 = (f32[9,1,10,1]{3,2,0,1:T(8,128)S(1)}, f32[9,1,10,1]{3,2,0,1:T(8,128)S(1)}, u32[]{:S(2)}, u32[]{:S(2)}) collective-permute-start(f32[9,1,10,1]{3,2,0,1:T(8,128)S(1)} %get-tuple-element.21), channel_id=1, source_target_pairs={{1,0},{3,2},{5,4},{7,6},{9,8},{11,10},{13,12},{15,14},{17,16},{19,... | collective-permute-start | bytes 1088 | tf_op jit(solution)/shard_map/ppermute | solution.py:20
  41.0 0.0 copy-done
  41.0 0.0 copy-done.1
  41.1 0.3 convolution_bitcast_fusion.1
  41.3 0.1 copy.13
  41.4 0.0 collective-permute-done.2
  41.4 1.6 %collective-permute-done.3 = f32[9,1,10,1]{3,2,0,1:T(8,128)S(1)} collective-permute-done((f32[9,1,10,1]{3,2,0,1:T(8,128)S(1)}, f32[9,1,10,1]{3,2,0,1:T(8,128)S(1)}, u32[]{:S(2)}, u32[]{:S(2)}) %collective-permute-start.3) | collective-permute-done | bytes 392 | tf_op jit(solution)/shard_map/ppermute | solution.py:20
  43.0 0.2 pad_maximum_fusion
  43.2 0.1 fusion.12
  43.4 0.3 convolution_bitcast_fusion
  43.7 0.1 pad_maximum_fusion.5
  43.8 0.3 convolution_bitcast_fusion.4
  44.0 0.3 convolution_bitcast_fusion.3
  44.4 0.1 or_bitcast_fusion
  44.4 15.2 %all-reduce.1 = (f32[5]{0:T(128)S(1)}, f32[5,5]{1,0:T(8,128)S(1)}, f32[5]{0:T(128)S(1)}, f32[5,5]{0,1:T(8,128)S(1)}) all-reduce(f32[5]{0:T(128)S(1)} %convolution_bitcast_fusion.4, f32[5,5]{1,0:T(8,128)S(1)} %convolution_bitcast_fusion.1, f32[5]{0:T(128)S(1)} %convolution_bitcast_fusion.3, ...), channel_id=1, replica_groups=mesh['shot'=4,'gx'=4,'gy'=2] {'gx','gy'}, use_global_device_ids=true, to_apply=%region_5.0 | all-reduce | flops 60 | bytes 480 | tf_op jit(solution)/shard_map/psum | solution.py:105
  59.7 11.9 %all-reduce.2 = (f32[5]{0:T(128)S(1)}, f32[5,5]{1,0:T(8,128)S(1)}, f32[5]{0:T(128)S(1)}, f32[5,5]{0,1:T(8,128)S(1)}) all-reduce(f32[5]{0:T(128)S(1)} %get-tuple-element.5, f32[5,5]{1,0:T(8,128)S(1)} %get-tuple-element.6, f32[5]{0:T(128)S(1)} %get-tuple-element.7, ...), channel_id=1, replica_groups=mesh['shot'=4,'gx'=4,'gy'=2] {'shot'}, use_global_device_ids=true, to_apply=%region_6.0 | all-reduce | flops 60 | bytes 480 | tf_op jit(solution)/shard_map/psum | solution.py:105
  71.6 0.7 fusion.28
  72.3 0.7 fusion.30
  82.4 0.6 gather_fusion
  86.4 0.1 stack.48
  86.5 0.1 fusion
  86.7 0.7 fusion.29
  100.1 0.1 stack.54
  100.2 0.2 fusion.1
  100.4 0.2 fusion.21
  100.7 0.6 negate_bitcast_fusion
  (8 shorter events, 0.2 us)
Async XLA Ops:
  6.5 20.8 %reduce-scatter.4.cloned.1.call-start = ((), (), s32[]{:S(2)}) async-start(), calls=%async_computation.1 | async-start | bytes 184320
  28.2 5.6 %collective-permute-start = (f32[9,1,1,128]{3,2,0,1:T(1,128)S(1)}, f32[9,1,1,128]{3,2,0,1:T(1,128)S(1)}, u32[]{:S(2)}, u32[]{:S(2)}) collective-permute-start(f32[9,1,1,128]{3,2,0,1:T(1,128)S(1)} %get-tuple-element.29), channel_id=1, source_target_pairs={{0,2},{2,4},{4,6},{1,3},{3,5},{5,7},{8,10},{10,12},{12,14},{9,11},... | collective-permute-start | bytes 13832 | tf_op jit(solution)/shard_map/ppermute | solution.py:18
  30.1 5.0 %collective-permute-start.1 = (f32[9,1,1,128]{3,2,0,1:T(1,128)S(1)}, f32[9,1,1,128]{3,2,0,1:T(1,128)S(1)}, u32[]{:S(2)}, u32[]{:S(2)}) collective-permute-start(f32[9,1,1,128]{3,2,0,1:T(1,128)S(1)} %get-tuple-element.30), channel_id=1, source_target_pairs={{2,0},{4,2},{6,4},{3,1},{5,3},{7,5},{10,8},{12,10},{14,12},{11,9},... | collective-permute-start | bytes 13832 | tf_op jit(solution)/shard_map/ppermute | solution.py:20
  35.1 6.0 %copy-start = (f32[5,3,1,8,128]{4,3,2,1,0:T(8,128)S(1)}, f32[5,3,1,8,128]{4,3,2,1,0:T(8,128)}, u32[]{:S(2)}) copy-start(f32[5,3,1,8,128]{4,3,2,1,0:T(8,128)} %param.5) | copy-start | bytes 184324
  35.1 6.0 %copy-start.1 = (f32[5,3,1,8,128]{4,3,2,1,0:T(8,128)S(1)}, f32[5,3,1,8,128]{4,3,2,1,0:T(8,128)}, u32[]{:S(2)}) copy-start(f32[5,3,1,8,128]{4,3,2,1,0:T(8,128)} %param.4) | copy-start | bytes 184324
  35.2 6.2 %collective-permute-start.2 = (f32[9,1,10,1]{3,2,0,1:T(8,128)S(1)}, f32[9,1,10,1]{3,2,0,1:T(8,128)S(1)}, u32[]{:S(2)}, u32[]{:S(2)}) collective-permute-start(f32[9,1,10,1]{3,2,0,1:T(8,128)S(1)} %get-tuple-element.20), channel_id=1, source_target_pairs={{0,1},{2,3},{4,5},{6,7},{8,9},{10,11},{12,13},{14,15},{16,17},{18,... | collective-permute-start | bytes 1088 | tf_op jit(solution)/shard_map/ppermute | solution.py:18
  36.5 6.5 %collective-permute-start.3 = (f32[9,1,10,1]{3,2,0,1:T(8,128)S(1)}, f32[9,1,10,1]{3,2,0,1:T(8,128)S(1)}, u32[]{:S(2)}, u32[]{:S(2)}) collective-permute-start(f32[9,1,10,1]{3,2,0,1:T(8,128)S(1)} %get-tuple-element.21), channel_id=1, source_target_pairs={{1,0},{3,2},{5,4},{7,6},{9,8},{11,10},{13,12},{15,14},{17,16},{19,... | collective-permute-start | bytes 1088 | tf_op jit(solution)/shard_map/ppermute | solution.py:20
Sparse Core Ops, SparseCore 0:
  9.6 17.7 reduce-scatter.3
